TPU v7x, 32 devices: a whole 2x2x4 slice. The times are simulated.
32 devices in a mesh: group: 1, path: 32 (over z, y, x, core).
Axes of the slice: x: 2, y: 2, z: 4, core: 2. Of those that a mesh axis runs over, the one named last changes fastest.
Arguments:
- normals: float32 [8, 32, 8192], P(None, None, ('group', 'path')), may hold values from -6 to 6
- start_state: float32 [32, 8192], P(None, ('group', 'path')), may hold values from -0.12 to 0.12
- later_adjoint: float32 [32, 8192], P(None, ('group', 'path')), may hold values from -1.8 to 1.8
- vol: float32 [8], replicated, may hold values from 0.004 to 0.016
- factor_load: float32 [32, 960], replicated, may hold values from -2.1 to 2.1
- knots: float32 [960], replicated, may hold values from 0.01 to 0.05
- spline_jac: float32 [960, 960], replicated
- cashflows: bfloat16 [256, 960], P(('group', 'path')), may hold values from -0.1875 to 0.1875
- trade_set: int32 [256, 1], P(('group', 'path')), may hold values from 0 to 127
- trade_end: int32 [256], P(('group', 'path')), may hold values from 240 to 960
- set_cpty: int32 [128, 1], P('group'), may hold values from 0 to 63
- default_prob: float32 [8, 64], replicated, may hold values from 0.01 to 0.1
- base_value: float32 [8, 128], P(None, 'group'), may hold values from -3 to 3
Outputs:
- knot_grad: float32 [960], P('group')
- alloc: float32 [256], P(('group', 'path'))
- start_adjoint: float32 [32, 8192], P(None, ('group', 'path'))
All inputs are finite; a program needn't handle non-finite values.
Results may differ from a plain program's by a relative error of at most 0.0011.
Values may be sent and summed in bfloat16 or wider, within the bound.
No kernel may reach another device: no remote copies, remote signals or barrier semaphores. Data moves between devices by JAX's collectives and lax.ppermute only.
A program may use at most 64 MiB of HBM per device.

v0:
```python
import math
import jax
import jax.numpy as jnp
from jax import lax
from jax.sharding import PartitionSpec as P

MEAN_REV = 0.05
STEP_YEARS = 0.25
HORIZON_YEARS = 30.0
SHARPNESS = 4.0
LOSS_RATE = 0.6


def curve_terms(knots, spline_jac, date_count, knot_count):
    zero_rate = jnp.dot(spline_jac, knots, precision=lax.Precision.HIGHEST)
    knot_index = jnp.arange(knot_count, dtype=jnp.int32)
    date_index = jnp.arange(date_count, dtype=jnp.int32)
    is_alive = 120 * (knot_index[None, :] + 1) > knot_count * (date_index[:, None] + 1)
    maturity = HORIZON_YEARS * (knot_index + 1).astype(jnp.float32) / knot_count
    fixing = STEP_YEARS * (date_index + 1).astype(jnp.float32)
    horizon = jnp.where(is_alive, maturity[None, :] - fixing[:, None], jnp.float32(0.0))
    loading = (1.0 - jnp.exp(-MEAN_REV * horizon)) / MEAN_REV
    discount = jnp.where(is_alive, jnp.exp(-zero_rate[None, :] * horizon), jnp.float32(0.0))
    return (horizon, loading, discount)


def state_path(start_state, vol, normals):
    decay_factor = math.exp(-MEAN_REV * STEP_YEARS)
    state = start_state
    collected = []
    for index in range(normals.shape[0]):
        state = decay_factor * state + vol[index] * normals[index]
        collected.append(state)
    return jnp.stack(collected)


def per_device(
    normals,
    start_state,
    later_adjoint,
    vol,
    factor_load,
    knots,
    spline_jac,
    cashflows,
    trade_set,
    trade_end,
    set_cpty,
    default_prob,
    base_value,
):
    highest = lax.Precision.HIGHEST
    date_count = normals.shape[0]
    knot_count = knots.shape[0]
    set_count = base_value.shape[1]
    paths_all = normals.shape[2] * lax.axis_size("path")
    horizon, loading, discount = curve_terms(knots, spline_jac, date_count, knot_count)
    knot_index = jnp.arange(knot_count, dtype=jnp.int32)
    live_flows = jnp.where(
        knot_index[None, :] < trade_end[:, None], cashflows, jnp.zeros_like(cashflows)
    )
    set_ids = trade_set[:, 0]
    labels = jnp.arange(set_count, dtype=jnp.int32)
    all_flows, all_sets = (
        lax.all_gather(live_flows, "path", axis=0, tiled=True),
        lax.all_gather(set_ids, "path", axis=0, tiled=True),
    )
    member = (labels[:, None] == all_sets[None, :]).astype(jnp.bfloat16)
    net_flows = jnp.dot(member, all_flows, preferred_element_type=jnp.float32).astype(jnp.bfloat16)
    counter = (
        jnp.arange(default_prob.shape[1], dtype=jnp.int32)[:, None] == set_cpty[:, 0][None, :]
    ).astype(jnp.float32)
    weight = LOSS_RATE * jnp.dot(default_prob, counter, precision=highest)
    states = state_path(start_state, vol, normals)
    shift = jnp.einsum("fm,ifp->imp", factor_load, states, precision=highest)
    bond_term = jnp.exp(-loading[:, :, None] * shift)
    feat_exact = discount[:, :, None] * bond_term
    features = feat_exact.astype(jnp.bfloat16)
    values = jnp.einsum("nm,imp->inp", net_flows, features, preferred_element_type=jnp.float32)
    mean_value = lax.psum(jnp.sum(values, axis=2), "path") / paths_all
    shifted = values - mean_value[:, :, None] + base_value[:, :, None]
    slope = weight[:, :, None] * jax.nn.sigmoid(SHARPNESS * shifted)
    mean_slope = lax.psum(jnp.sum(slope, axis=2), "path") / paths_all
    set_adjoint = (slope - mean_slope[:, :, None]).astype(jnp.bfloat16)
    feat_adjoint = jnp.einsum(
        "nm,inp->imp", net_flows, set_adjoint, preferred_element_type=jnp.float32
    )
    state_local = -jnp.einsum(
        "fm,imp->ifp",
        factor_load,
        feat_adjoint * feat_exact * loading[:, :, None],
        precision=highest,
    )
    discount_grad = jnp.sum(feat_adjoint * bond_term, axis=2)
    rate_adjoint = -jnp.sum(discount_grad * discount * horizon, axis=0) / paths_all
    rate_total = lax.psum(rate_adjoint, "path")
    knot_grad = jnp.dot(spline_jac.T, rate_total, precision=highest)
    load_sums = (
        jnp.einsum("inp,imp->nm", set_adjoint, features, preferred_element_type=jnp.float32)
        / paths_all
    )
    set_rows = load_sums[all_sets]
    trade_part = jnp.sum(all_flows.astype(jnp.float32) * set_rows, axis=1)
    alloc = lax.psum_scatter(trade_part, "path", scatter_dimension=0, tiled=True)
    decay_factor = math.exp(-MEAN_REV * STEP_YEARS)
    carried = later_adjoint + state_local[date_count - 1]
    for index in reversed(range(date_count - 1)):
        carried = state_local[index] + decay_factor * carried
    start_adjoint = decay_factor * carried
    return (knot_grad, alloc, start_adjoint)


def solution(mesh):
    in_specs = (
        P(None, None, ("group", "path")),
        P(None, ("group", "path")),
        P(None, ("group", "path")),
        P(),
        P(),
        P(),
        P(),
        P(("group", "path"), None),
        P(("group", "path"), None),
        P(("group", "path")),
        P("group", None),
        P(),
        P(None, "group"),
    )
    out_specs = (P("group"), P(("group", "path")), P(None, ("group", "path")))
    return jax.shard_map(
        per_device, mesh=mesh, in_specs=in_specs, out_specs=out_specs, check_vma=False
    )
```

profile of v0, /device:TPU:0, one launch (start us, length us, event | category | flops | bytes accessed | tf_op | source)
XLA Modules:
  0.0 270.6 jit_solution(15762425865365894682)
XLA Ops:
  0.6 0.0 copy-start
  0.7 0.0 copy-start.16
  0.7 0.0 copy-start.18
  0.7 0.8 bitcast_dynamic-update-slice_fusion.8
  1.5 41.9 %all-reduce = s32[256]{0:T(256)S(1)} all-reduce(s32[256]{0:T(256)S(1)} %bitcast_dynamic-update-slice_fusion.8), channel_id=2, replica_groups=mesh['group'=1,'path'=32] {'path'}, use_global_device_ids=true, to_apply=%add | all-reduce | flops 256 | bytes 2048 | tf_op jit(solution)/shard_map/all_gather | solution.py:66
  43.4 0.6 pad_clamp_fusion
  44.0 0.8 fusion.18
  44.8 0.0 copy-start.5
  44.9 0.0 copy-start.7
  44.9 5.4 %fusion.50 = f32[1,960]{1,0:T(1,128)S(1)} fusion(f32[960,960]{1,0:T(8,128)} %param.19, f32[960,1]{0,1:T(1,128)} %bitcast.192), kind=kOutput, calls=%fused_computation.96 | convolution fusion | flops 11059200 | bytes 3694080 | tf_op jit(solution)/shard_map/dot_general | solution.py:15
  50.3 1.6 fusion.48
  52.0 0.8 fusion.42
  52.8 0.7 subtract_multiply_fusion
  53.5 1.5 bitcast_dynamic-update-slice_fusion.7
  54.9 2.0 bitcast_dynamic-update-slice_fusion.6
  57.0 1.5 bitcast_dynamic-update-slice_fusion.5
  58.4 2.0 bitcast_dynamic-update-slice_fusion.4
  60.5 1.5 bitcast_dynamic-update-slice_fusion.3
  61.9 2.1 bitcast_dynamic-update-slice_fusion.2
  64.1 1.4 bitcast_dynamic-update-slice_fusion.1
  65.4 2.1 bitcast_dynamic-update-slice_fusion
  67.5 41.7 %all_gather.7 = bf16[256,960]{1,0:T(8,128)(2,1)S(1)} all-gather(bf16[8,960]{1,0:T(8,128)(2,1)S(1)} %fusion.42), channel_id=1, replica_groups=mesh['group'=1,'path'=32] {'path'}, dimensions={0}, use_global_device_ids=true | all-gather | bytes 506880 | tf_op jit(solution)/shard_map/all_gather | solution.py:65
  109.2 0.3 fusion.17
  109.6 0.0 copy-done
  109.6 0.0 copy-start.13
  109.6 6.5 %fusion.23 = f32[8,256,960]{1,2,0:T(8,128)S(1)} fusion(f32[8,32,256]{2,1,0:T(8,128)S(1)} %bitcast_dynamic-update-slice_fusion, f32[32,960]{1,0:T(8,128)S(1)} %copy-done), kind=kOutput, calls=%fused_computation.28 | convolution fusion | flops 754974720 | bytes 8249344 | tf_op jit(solution)/shard_map/fm,ifp->imp/dot_general | solution.py:75
  116.1 0.0 copy-start.1
  116.1 3.1 %copy-done.1 = f32[8,256,960]{1,2,0:T(8,128)} copy-done((f32[8,256,960]{1,2,0:T(8,128)}, f32[8,256,960]{1,2,0:T(8,128)S(1)}, u32[]{:S(2)}) %copy-start.1) | copy-done | bytes 7864344
  119.1 5.4 %fusion.49 = (f32[8,128]{1,0:T(8,128)S(1)}, f32[8,128,256]{1,2,0:T(8,128)S(1)}) fusion(bf16[128,960,1]{0,1,2:T(8,128)(2,1)S(1)} %fusion.17, f32[8,256,960]{1,2,0:T(8,128)S(1)} %fusion.23, f32[8,960]{1,0:T(8,128)S(1)} %get-tuple-element.12, f32[8,960]{1,0:T(8,128)S(1)} %get-tuple-element.13), kind=kOutput, calls=%fused_computation.95 | convolution fusion | flops 509475840 | bytes 9224192 | tf_op jit(solution)/shard_map/nm,imp->inp/dot_general | solution.py:79
  124.5 0.0 copy-done.16
  124.6 0.0 copy-done.18
  124.6 0.0 copy-done.5
  124.6 0.0 copy-done.7
  124.6 0.0 copy-done.9
  124.6 37.0 %psum.21 = f32[8,128]{1,0:T(8,128)S(1)} all-reduce(f32[8,128]{1,0:T(8,128)S(1)} %get-tuple-element.22), channel_id=1, replica_groups=mesh['group'=1,'path'=32] {'path'}, use_global_device_ids=true, to_apply=%region_1.2 | all-reduce | flops 1024 | bytes 8192 | tf_op jit(solution)/shard_map/psum | solution.py:80
  161.6 0.0 copy-done.13
  161.6 0.3 fusion.47
  162.0 41.2 %psum.22 = f32[8,128]{1,0:T(8,128)S(1)} all-reduce(f32[8,128]{1,0:T(8,128)S(1)} %fusion.47), channel_id=1, replica_groups=mesh['group'=1,'path'=32] {'path'}, use_global_device_ids=true, to_apply=%region_3.4 | all-reduce | flops 1024 | bytes 8192 | tf_op jit(solution)/shard_map/psum | solution.py:83
  203.1 0.0 copy-done.14
  203.1 0.0 copy-done.11
  203.2 0.0 copy-start.15
  203.2 0.6 copy-done.15
  203.8 5.4 %fusion.10 = f32[128,960]{0,1:T(8,128)S(1)} fusion(f32[8,256,960]{1,2,0:T(8,128)} %copy-done.1, f32[8,960]{1,0:T(8,128)S(1)} %get-tuple-element.12, f32[8,960]{1,0:T(8,128)S(1)} %get-tuple-element.13, f32[8,128]{1,0:T(8,128)S(1)} %broadcast_multiply_fusion, f32[8,128,256]{1,2,0:T(8,128)S(1)} %get-tuple-element.23, f32[8,128]{1,0:T(8,128)S(1)} %copy-done.13, ...), kind=kOutput, calls=%fused_computation.16 | convolution fusion | flops 511696896 | bytes 9482240 | tf_op jit(solution)/shard_map/inp,imp->nm/dot_general | solution.py:99
  209.2 0.2 copy.21
  209.4 1.2 gather_fusion
  210.6 0.0 slice-start
  210.6 0.2 multiply_reduce_fusion
  210.8 0.0 copy-start.3
  210.8 0.0 copy-start.4
  210.8 6.4 %fusion = (f32[8,960]{1,0:T(8,128)S(1)}, f32[8,256,960]{1,2,0:T(8,128)S(1)}) fusion(f32[8,256,960]{1,2,0:T(8,128)} %copy-done.1, f32[8,960]{1,0:T(8,128)S(1)} %get-tuple-element.12, bf16[128,960,1]{0,1,2:T(8,128)(2,1)S(1)} %fusion.17, f32[8,128]{1,0:T(8,128)} %copy-done.15, f32[8,128]{1,0:T(8,128)} %param.25, f32[8,128,256]{1,2,0:T(8,128)S(1)} %get-tuple-element.23, ...), kind=kOutput, calls=%fused_computation.3 | convolution fusion | flops 511566336 | bytes 17100800 | tf_op jit(solution)/shard_map/nm,inp->imp/dot_general | solution.py:85
  217.3 0.0 copy-start.12
  217.3 0.0 copy-start.6
  217.3 0.0 copy-start.8
  217.3 0.0 copy-start.10
  217.3 0.0 copy-start.17
  217.4 0.0 copy-start.19
  217.4 7.6 %fusion.14 = f32[8,32,256]{2,1,0:T(8,128)S(1)} fusion(f32[8,256,960]{1,2,0:T(8,128)S(1)} %get-tuple-element.25, f32[8,256,960]{1,2,0:T(8,128)S(1)} %bitcast.190, f32[8,960]{1,0:T(8,128)S(1)} %copy-done.4, f32[8,960]{1,0:T(8,128)S(1)} %get-tuple-element.12, f32[8,960]{1,0:T(8,128)S(1)} %copy-done.3, f32[32,960]{1,0:T(8,128)S(1)} %copy-done), kind=kOutput, calls=%fused_computation.19 | convolution fusion | flops 762904576 | bytes 16205824 | tf_op jit(solution)/shard_map/fm,imp->ifp/dot_general | solution.py:88
  224.9 0.0 copy-done.12
  225.0 0.6 fusion.41
  225.6 0.0 copy-done.8
  225.6 0.1 multiply_reduce_fusion.1
  225.7 39.6 %all-reduce.2 = (f32[960]{0:T(1024)S(1)}, f32[256]{0:T(256)S(1)}) all-reduce(f32[960]{0:T(1024)S(1)} %negate_multiply_fusion, f32[256]{0:T(256)S(1)} %multiply_reduce_fusion), channel_id=1, replica_groups=mesh['group'=1,'path'=32] {'path'}, use_global_device_ids=true, to_apply=%region_6.7 | all-reduce | flops 1216 | bytes 9728 | tf_op jit(solution)/shard_map/psum | solution.py:96
  265.3 4.7 %fusion.5 = f32[1,960]{1,0:T(1,128)} fusion(f32[960,1]{0,1:T(1,128)S(1)} %bitcast.194, f32[960,960]{1,0:T(8,128)} %param.19), kind=kOutput, calls=%fused_computation.9 | convolution fusion | flops 11059200 | bytes 3694080 | tf_op jit(solution)/shard_map/dot_general | solution.py:97
  270.0 0.6 dynamic-slice
  (25 shorter events, 0.1 us)
Async XLA Ops:
  0.6 108.9 %copy-start = (f32[32,960]{1,0:T(8,128)S(1)}, f32[32,960]{1,0:T(8,128)}, u32[]{:S(2)}) copy-start(f32[32,960]{1,0:T(8,128)} %param.17) | copy-start | bytes 368644
  0.7 123.9 %copy-start.16 = (s32[8]{0:T(128)}, s32[8]{0:T(128)S(1)}, u32[]{:S(2)}) copy-start(s32[8]{0:T(128)S(1)} %fusion.46) | copy-start | bytes 100
  0.7 123.9 %copy-start.18 = (f32[8]{0:T(128)}, f32[8]{0:T(128)S(1)}, u32[]{:S(2)}) copy-start(f32[8]{0:T(128)S(1)} %convert_multiply_fusion.1) | copy-start | bytes 100
  44.8 158.3 %copy-start.14 = (f32[8,128]{1,0:T(8,128)}, f32[8,128]{1,0:T(8,128)S(1)}, u32[]{:S(2)}) copy-start(f32[8,128]{1,0:T(8,128)S(1)} %fusion.18) | copy-start | bytes 12292
  44.8 79.7 %copy-start.5 = (s32[960]{0:T(1024)}, s32[960]{0:T(1024)S(1)}, u32[]{:S(2)}) copy-start(s32[960]{0:T(1024)S(1)} %fusion.44) | copy-start | bytes 11524
  44.9 79.7 %copy-start.7 = (f32[960]{0:T(1024)}, f32[960]{0:T(1024)S(1)}, u32[]{:S(2)}) copy-start(f32[960]{0:T(1024)S(1)} %convert_multiply_fusion) | copy-start | bytes 11524
  50.3 74.3 %copy-start.9 = (f32[960]{0:T(1024)}, f32[960]{0:T(1024)S(1)}, u32[]{:S(2)}) copy-start(f32[960]{0:T(1024)S(1)} %neg.24) | copy-start | bytes 11524
  53.5 149.7 %copy-start.2 = (f32[8,960]{1,0:T(8,128)}, f32[8,960]{1,0:T(8,128)S(1)}, u32[]{:S(2)}) copy-start(f32[8,960]{1,0:T(8,128)S(1)} %get-tuple-element.13) | copy-start | bytes 92164
  109.6 52.1 %copy-start.13 = (f32[8,128]{1,0:T(8,128)S(1)}, f32[8,128]{1,0:T(8,128)}, u32[]{:S(2)}) copy-start(f32[8,128]{1,0:T(8,128)} %param.25) | copy-start | bytes 12292
  116.1 3.1 %copy-start.1 = (f32[8,256,960]{1,2,0:T(8,128)}, f32[8,256,960]{1,2,0:T(8,128)S(1)}, u32[]{:S(2)}) copy-start(f32[8,256,960]{1,2,0:T(8,128)S(1)} %fusion.23) | copy-start | bytes 23592964
  161.6 41.5 %copy-start.11 = (f32[8,128]{1,0:T(8,128)}, f32[8,128]{1,0:T(8,128)S(1)}, u32[]{:S(2)}) copy-start(f32[8,128]{1,0:T(8,128)S(1)} %broadcast_multiply_fusion.1) | copy-start | bytes 12292
  203.2 0.6 copy-start.15
  210.6 6.7 %slice-start = ((s8[7864320]{0:T(1024)(128)(4,1)}), s8[4194304]{0:T(1024)(128)(4,1)S(1)}, s32[]{:S(2)}) async-start(s8[7864320]{0:T(1024)(128)(4,1)} %bitcast.189), calls=%async_computation | async-start | bytes 8388608
  210.8 6.5 %slice-start.1 = ((s8[7864320]{0:T(1024)(128)(4,1)}), s8[3670016]{0:T(1024)(128)(4,1)S(1)}, s32[]{:S(2)}) async-start(s8[7864320]{0:T(1024)(128)(4,1)} %bitcast.189), calls=%async_computation.1 | async-start | bytes 7340032
  210.8 6.5 %copy-start.3 = (f32[8,960]{1,0:T(8,128)S(1)}, f32[8,960]{1,0:T(8,128)}, u32[]{:S(2)}) copy-start(f32[8,960]{1,0:T(8,128)} %copy-done.2) | copy-start | bytes 92164
  210.8 6.5 %copy-start.4 = (f32[8,960]{1,0:T(8,128)S(1)}, f32[8,960]{1,0:T(8,128)}, u32[]{:S(2)}) copy-start(f32[8,960]{1,0:T(8,128)} %get-tuple-element.11) | copy-start | bytes 92164
  217.3 7.6 %copy-start.12 = (f32[32,256]{1,0:T(8,128)S(1)}, f32[32,256]{1,0:T(8,128)}, u32[]{:S(2)}) copy-start(f32[32,256]{1,0:T(8,128)} %param.15) | copy-start | bytes 98308
  217.3 8.3 %copy-start.6 = (s32[960]{0:T(1024)S(1)}, s32[960]{0:T(1024)}, u32[]{:S(2)}) copy-start(s32[960]{0:T(1024)} %copy-done.5) | copy-start | bytes 11524
  217.3 8.3 %copy-start.8 = (f32[960]{0:T(1024)S(1)}, f32[960]{0:T(1024)}, u32[]{:S(2)}) copy-start(f32[960]{0:T(1024)} %copy-done.7) | copy-start | bytes 11524
  217.3 8.3 %copy-start.10 = (f32[960]{0:T(1024)S(1)}, f32[960]{0:T(1024)}, u32[]{:S(2)}) copy-start(f32[960]{0:T(1024)} %copy-done.9) | copy-start | bytes 11524
  217.3 8.3 %copy-start.17 = (s32[8]{0:T(128)S(1)}, s32[8]{0:T(128)}, u32[]{:S(2)}) copy-start(s32[8]{0:T(128)} %copy-done.16) | copy-start | bytes 100
  217.4 8.3 %copy-start.19 = (f32[8]{0:T(128)S(1)}, f32[8]{0:T(128)}, u32[]{:S(2)}) copy-start(f32[8]{0:T(128)} %copy-done.18) | copy-start | bytes 100
where the time goes:
time: 272 us; the launch traced here: 271 us
  blocking collectives  201 us (74%)
  matrix products  42.6 us (16%)
  other arithmetic  17.4 us (6%)
  local copies, waits for them, and re-layouts  8.13 us (3%)
    all_gather x1, blocking collectives, per_device(): lax.all_gather(set_ids, 'path', axis=0, tiled=True)  41.9 us
    all_gather x1, blocking collectives, per_device(): lax.all_gather(live_flows, 'path', axis=0, tiled=True)  41.7 us
    psum x1, blocking collectives, per_device(): mean_slope = lax.psum(jnp.sum(slope, axis=2), 'path') / paths_all  41.2 us
    psum x1, blocking collectives, per_device(): rate_total = lax.psum(rate_adjoint, 'path')  39.6 us
    psum x1, blocking collectives, per_device(): mean_value = lax.psum(jnp.sum(values, axis=2), 'path') / paths_all  37 us
    unnamed x8, other arithmetic  12 us
    dot_general x1, matrix products, per_device(): jnp.einsum('fm,imp->ifp', factor_load, feat_adjoint * feat_exact * loadin...  7.57 us
    dot_general x1, matrix products, per_device(): shift = jnp.einsum('fm,ifp->imp', factor_load, states, precision=highest)  6.46 us

commit v1 on v0

--- a/solution.py
+++ b/solution.py
@@ -9,6 +9,18 @@
 HORIZON_YEARS = 30.0
 SHARPNESS = 4.0
 LOSS_RATE = 0.6
+
+
+def doubled_up(x, axis, dim):
+    ways, here = (lax.axis_size(axis), lax.axis_index(axis))
+    grown, reach = (x, 1)
+    while reach < ways:
+        theirs = lax.ppermute(grown, axis, [(d, d ^ reach) for d in range(ways)])
+        mine_first = jnp.concatenate([grown, theirs], axis=dim)
+        theirs_first = jnp.concatenate([theirs, grown], axis=dim)
+        grown = jnp.where(here & reach == 0, mine_first, theirs_first)
+        reach = 2 * reach
+    return grown
 
 
 def curve_terms(knots, spline_jac, date_count, knot_count):
@@ -62,7 +74,7 @@
     set_ids = trade_set[:, 0]
     labels = jnp.arange(set_count, dtype=jnp.int32)
     all_flows, all_sets = (
-        lax.all_gather(live_flows, "path", axis=0, tiled=True),
+        doubled_up(live_flows, "path", 0),
         lax.all_gather(set_ids, "path", axis=0, tiled=True),
     )
     member = (labels[:, None] == all_sets[None, :]).astype(jnp.bfloat16)

time: 272 us -> 258 us (0.949)
  blocking collectives: 201 us -> 160 us
  waiting for transfers between devices: 0 us -> 16.9 us
  starting transfers between devices: 0 us -> 8.76 us
  matrix products: 42.6 us -> 49.9 us
  local copies, waits for them, and re-layouts: 8.13 us -> 4.23 us
    all_gather x1 -> x0, blocking collectives: 41.7 us -> none  [per_device(): lax.all_gather(live_flows, 'path', axis=0, tiled=True)]
    ppermute x0 -> x5, waiting for transfers between devices: none -> 16.9 us  [doubled_up(): theirs = lax.ppermute(grown, axis, [(d, d ^ reach) for d in range(ways)])]
    ppermute x0 -> x5, starting transfers between devices: none -> 8.76 us  [doubled_up(): theirs = lax.ppermute(grown, axis, [(d, d ^ reach) for d in range(ways)])]
    unnamed x47 -> x9, local copies, waits for them, and re-layouts: 5.08 us -> 1.34 us
    dot_general x1, matrix products: 7.57 us -> 11 us  [per_device(): jnp.einsum('fm,imp->ifp', factor_load, feat_adjoint * feat_exact * loadin...]
    unnamed x8 -> x7, other arithmetic: 12 us -> 11.7 us
  transfers between devices with their start and end apart: 0 -> 5, of which waited for: 0 -> 4; matrix products, arithmetic and copies ran while one was open for 0% -> 12% of each run, Pallas kernels for 0% -> 0%
where the time goes in v1:
time: 258 us; the launch traced here: 257 us
  blocking collectives  160 us (62%)
  matrix products  49.9 us (19%)
  waiting for transfers between devices  16.9 us (7%)
  other arithmetic  16.1 us (6%)
  starting transfers between devices  8.76 us (3%)
  local copies, waits for them, and re-layouts  4.23 us (2%)
    psum x1, blocking collectives, per_device(): mean_slope = lax.psum(jnp.sum(slope, axis=2), 'path') / paths_all  42.3 us
    all_gather x1, blocking collectives, per_device(): lax.all_gather(set_ids, 'path', axis=0, tiled=True)  41.5 us
    psum x1, blocking collectives, per_device(): mean_value = lax.psum(jnp.sum(values, axis=2), 'path') / paths_all  38.3 us
    psum x1, blocking collectives, per_device(): rate_total = lax.psum(rate_adjoint, 'path')  38.1 us
    ppermute x5, waiting for transfers between devices, doubled_up(): theirs = lax.ppermute(grown, axis, [(d, d ^ reach) for d in range(ways)])  16.9 us
    unnamed x7, other arithmetic  11.7 us
    dot_general x1, matrix products, per_device(): jnp.einsum('fm,imp->ifp', factor_load, feat_adjoint * feat_exact * loadin...  11 us
    ppermute x5, starting transfers between devices, doubled_up(): theirs = lax.ppermute(grown, axis, [(d, d ^ reach) for d in range(ways)])  8.76 us
  transfers between devices with their start and end apart: 5, of which 4 were waited for; matrix products, arithmetic and copies ran while one was open for 12% of the time, Pallas kernels for 0%

profile of v1, /device:TPU:0, one launch (start us, length us, event | category | flops | bytes accessed | tf_op | source)
XLA Modules:
  0.0 256.8 jit_solution(3887648041533514649)
XLA Ops:
  0.6 0.0 copy-start
  0.6 0.8 fusion.42
  1.5 0.5 collective-permute-start
  2.0 0.7 bitcast_dynamic-update-slice_fusion.8
  2.7 41.5 %all-reduce = s32[256]{0:T(256)S(1)} all-reduce(s32[256]{0:T(256)S(1)} %bitcast_dynamic-update-slice_fusion.8), channel_id=2, replica_groups=mesh['group'=1,'path'=32] {'path'}, use_global_device_ids=true, to_apply=%add | all-reduce | flops 256 | bytes 2048 | tf_op jit(solution)/shard_map/all_gather | solution.py:78
  44.2 1.6 fusion.49
  45.8 0.8 fusion.18
  46.7 5.5 %fusion.51 = f32[1,960]{1,0:T(1,128)S(1)} fusion(f32[960,960]{1,0:T(8,128)} %param.19, f32[960,1]{0,1:T(1,128)} %bitcast.189), kind=kOutput, calls=%fused_computation.102 | convolution fusion | flops 11059200 | bytes 3694080 | tf_op jit(solution)/shard_map/dot_general | solution.py:27
  52.1 1.4 bitcast_dynamic-update-slice_fusion.7
  53.5 2.1 bitcast_dynamic-update-slice_fusion.6
  55.6 1.3 bitcast_dynamic-update-slice_fusion.5
  56.9 2.0 bitcast_dynamic-update-slice_fusion.4
  59.0 1.4 bitcast_dynamic-update-slice_fusion.3
  60.4 2.1 bitcast_dynamic-update-slice_fusion.2
  62.5 1.4 bitcast_dynamic-update-slice_fusion.1
  63.8 2.0 bitcast_dynamic-update-slice_fusion
  65.9 0.0 copy-done
  65.9 8.5 %fusion.23 = f32[8,256,960]{1,2,0:T(8,128)} fusion(f32[8,32,256]{2,1,0:T(8,128)S(1)} %bitcast_dynamic-update-slice_fusion, f32[32,960]{1,0:T(8,128)S(1)} %copy-done), kind=kOutput, calls=%fused_computation.31 | convolution fusion | flops 754974720 | bytes 8249344 | tf_op jit(solution)/shard_map/fm,ifp->imp/dot_general | solution.py:87
  74.4 0.0 copy-start.2
  74.4 0.0 collective-permute-done
  74.4 2.3 collective-permute-start.1
  76.8 1.9 collective-permute-done.1
  78.7 2.1 collective-permute-start.2
  80.8 2.2 collective-permute-done.2
  83.0 1.6 collective-permute-start.3
  84.6 5.0 %collective-permute-done.3 = bf16[64,960]{1,0:T(8,128)(2,1)S(1)} collective-permute-done((bf16[64,960]{1,0:T(8,128)(2,1)S(1)}, bf16[64,960]{1,0:T(8,128)(2,1)S(1)}, u32[]{:S(2)}, u32[]{:S(2)}) %collective-permute-start.3) | collective-permute-done | bytes 122912 | tf_op jit(solution)/shard_map/ppermute | solution.py:18
  89.6 0.1 maximum_select_fusion.1
  89.7 2.3 collective-permute-start.4
  91.9 0.1 subtract_multiply_fusion
  92.0 7.8 %collective-permute-done.4 = bf16[128,960]{1,0:T(8,128)(2,1)S(1)} collective-permute-done((bf16[128,960]{1,0:T(8,128)(2,1)S(1)}, bf16[128,960]{1,0:T(8,128)(2,1)S(1)}, u32[]{:S(2)}, u32[]{:S(2)}) %collective-permute-start.4) | collective-permute-done | bytes 245792 | tf_op jit(solution)/shard_map/ppermute | solution.py:18
  99.8 0.3 fusion.17
  100.1 6.6 %fusion.50 = (f32[8,128]{1,0:T(8,128)S(1)}, f32[8,128,256]{1,2,0:T(8,128)S(1)}) fusion(bf16[128,960,1]{0,1,2:T(8,128)(2,1)S(1)} %fusion.17, f32[8,256,960]{1,2,0:T(8,128)} %fusion.23, f32[8,960]{1,0:T(8,128)S(1)} %get-tuple-element.12, f32[8,960]{1,0:T(8,128)S(1)} %get-tuple-element.13), kind=kOutput, calls=%fused_computation.101 | convolution fusion | flops 509475840 | bytes 9224192 | tf_op jit(solution)/shard_map/nm,imp->inp/dot_general | solution.py:91
  106.7 38.3 %psum.21 = f32[8,128]{1,0:T(8,128)S(1)} all-reduce(f32[8,128]{1,0:T(8,128)S(1)} %get-tuple-element.22), channel_id=1, replica_groups=mesh['group'=1,'path'=32] {'path'}, use_global_device_ids=true, to_apply=%region_1.2 | all-reduce | flops 1024 | bytes 8192 | tf_op jit(solution)/shard_map/psum | solution.py:92
  145.1 0.0 copy-done.2
  145.1 0.3 fusion.48
  145.4 42.3 %psum.22 = f32[8,128]{1,0:T(8,128)S(1)} all-reduce(f32[8,128]{1,0:T(8,128)S(1)} %fusion.48), channel_id=1, replica_groups=mesh['group'=1,'path'=32] {'path'}, use_global_device_ids=true, to_apply=%region_3.4 | all-reduce | flops 1024 | bytes 8192 | tf_op jit(solution)/shard_map/psum | solution.py:95
  187.6 5.4 %fusion.10 = f32[128,960]{0,1:T(8,128)S(1)} fusion(f32[8,256,960]{1,2,0:T(8,128)} %fusion.23, f32[8,960]{1,0:T(8,128)S(1)} %get-tuple-element.12, f32[8,960]{1,0:T(8,128)S(1)} %get-tuple-element.13, f32[8,128]{1,0:T(8,128)S(1)} %broadcast_multiply_fusion, f32[8,128,256]{1,2,0:T(8,128)S(1)} %get-tuple-element.23, f32[8,128]{1,0:T(8,128)S(1)} %copy-done.2, ...), kind=kOutput, calls=%fused_computation.16 | convolution fusion | flops 511696896 | bytes 9482240 | tf_op jit(solution)/shard_map/inp,imp->nm/dot_general | solution.py:111
  193.1 7.1 %fusion = (f32[8,960]{1,0:T(8,128)S(1)}, f32[8,256,960]{1,2,0:T(8,128)}) fusion(f32[8,256,960]{1,2,0:T(8,128)} %fusion.23, f32[8,960]{1,0:T(8,128)S(1)} %get-tuple-element.12, bf16[128,960,1]{0,1,2:T(8,128)(2,1)S(1)} %fusion.17, f32[8,128]{1,0:T(8,128)S(1)} %broadcast_multiply_fusion, f32[8,128]{1,0:T(8,128)S(1)} %copy-done.2, ...), kind=kOutput, calls=%fused_computation.3 | convolution fusion | flops 511566336 | bytes 17100800 | tf_op jit(solution)/shard_map/nm,inp->imp/dot_general | solution.py:97
  200.1 0.2 copy.21
  200.3 0.1 multiply_reduce_fusion.1
  200.4 1.1 gather_fusion
  201.5 0.2 multiply_reduce_fusion
  201.7 38.1 %all-reduce.2 = (f32[960]{0:T(1024)S(1)}, f32[256]{0:T(256)S(1)}) all-reduce(f32[960]{0:T(1024)S(1)} %negate_multiply_fusion, f32[256]{0:T(256)S(1)} %multiply_reduce_fusion), channel_id=1, replica_groups=mesh['group'=1,'path'=32] {'path'}, use_global_device_ids=true, to_apply=%region_6.7 | all-reduce | flops 1216 | bytes 9728 | tf_op jit(solution)/shard_map/psum | solution.py:108
  239.9 4.7 %fusion.5 = f32[1,960]{1,0:T(1,128)} fusion(f32[960,1]{0,1:T(1,128)S(1)} %bitcast.191, f32[960,960]{1,0:T(8,128)} %param.19), kind=kOutput, calls=%fused_computation.9 | convolution fusion | flops 11059200 | bytes 3694080 | tf_op jit(solution)/shard_map/dot_general | solution.py:109
  244.5 0.0 copy-start.1
  244.5 11.0 %fusion.14 = f32[8,32,256]{2,1,0:T(8,128)S(1)} fusion(f32[8,256,960]{1,2,0:T(8,128)} %get-tuple-element.25, f32[8,256,960]{1,2,0:T(8,128)} %fusion.23, f32[8,960]{1,0:T(8,128)S(1)} %get-tuple-element.11, f32[8,960]{1,0:T(8,128)S(1)} %get-tuple-element.12, f32[8,960]{1,0:T(8,128)S(1)} %get-tuple-element.13, f32[32,960]{1,0:T(8,128)S(1)} %copy-done), kind=kOutput, calls=%fused_computation.19 | convolution fusion | flops 762904576 | bytes 16205824 | tf_op jit(solution)/shard_map/fm,imp->ifp/dot_general | solution.py:100
  255.6 0.0 copy-done.1
  255.6 0.6 fusion.41
  256.2 0.6 dynamic-slice
  (14 shorter events, 0.1 us)
Async XLA Ops:
  0.6 65.3 %copy-start = (f32[32,960]{1,0:T(8,128)S(1)}, f32[32,960]{1,0:T(8,128)}, u32[]{:S(2)}) copy-start(f32[32,960]{1,0:T(8,128)} %param.17) | copy-start | bytes 368644
  1.5 72.9 %collective-permute-start = (bf16[8,960]{1,0:T(8,128)(2,1)S(1)}, bf16[8,960]{1,0:T(8,128)(2,1)S(1)}, u32[]{:S(2)}, u32[]{:S(2)}) collective-permute-start(bf16[8,960]{1,0:T(8,128)(2,1)S(1)} %fusion.42), channel_id=1, source_target_pairs={{0,1},{1,0},{2,3},{3,2},{4,5},{5,4},{6,7},{7,6},{8,9},{9,8},{10,11... | collective-permute-start | bytes 46088 | tf_op jit(solution)/shard_map/ppermute | solution.py:18
  74.4 70.7 %copy-start.2 = (f32[8,128]{1,0:T(8,128)S(1)}, f32[8,128]{1,0:T(8,128)}, u32[]{:S(2)}) copy-start(f32[8,128]{1,0:T(8,128)} %param.25) | copy-start | bytes 12292
  74.4 4.2 %collective-permute-start.1 = (bf16[16,960]{1,0:T(8,128)(2,1)S(1)}, bf16[16,960]{1,0:T(8,128)(2,1)S(1)}, u32[]{:S(2)}, u32[]{:S(2)}) collective-permute-start(bf16[16,960]{1,0:T(8,128)(2,1)S(1)} %maximum_select_fusion.5), channel_id=1, source_target_pairs={{0,2},{1,3},{2,0},{3,1},{4,6},{5,7},{6,4},{7,5},{8,10},{9,11},{10,... | collective-permute-start | bytes 92168 | tf_op jit(solution)/shard_map/ppermute | solution.py:18
  78.7 4.3 %collective-permute-start.2 = (bf16[32,960]{1,0:T(8,128)(2,1)S(1)}, bf16[32,960]{1,0:T(8,128)(2,1)S(1)}, u32[]{:S(2)}, u32[]{:S(2)}) collective-permute-start(bf16[32,960]{1,0:T(8,128)(2,1)S(1)} %maximum_select_fusion.4), channel_id=1, source_target_pairs={{0,4},{1,5},{2,6},{3,7},{4,0},{5,1},{6,2},{7,3},{8,12},{9,13},{10,... | collective-permute-start | bytes 184328 | tf_op jit(solution)/shard_map/ppermute | solution.py:18
  83.0 6.6 %collective-permute-start.3 = (bf16[64,960]{1,0:T(8,128)(2,1)S(1)}, bf16[64,960]{1,0:T(8,128)(2,1)S(1)}, u32[]{:S(2)}, u32[]{:S(2)}) collective-permute-start(bf16[64,960]{1,0:T(8,128)(2,1)S(1)} %maximum_select_fusion.2), channel_id=1, source_target_pairs={{0,8},{1,9},{2,10},{3,11},{4,12},{5,13},{6,14},{7,15},{8,0},{9,1},... | collective-permute-start | bytes 368648 | tf_op jit(solution)/shard_map/ppermute | solution.py:18
  89.7 10.1 %collective-permute-start.4 = (bf16[128,960]{1,0:T(8,128)(2,1)S(1)}, bf16[128,960]{1,0:T(8,128)(2,1)S(1)}, u32[]{:S(2)}, u32[]{:S(2)}) collective-permute-start(bf16[128,960]{1,0:T(8,128)(2,1)S(1)} %maximum_select_fusion.1), channel_id=1, source_target_pairs={{0,16},{1,17},{2,18},{3,19},{4,20},{5,21},{6,22},{7,23},{8,24},{9,... | collective-permute-start | bytes 737288 | tf_op jit(solution)/shard_map/ppermute | solution.py:18
  244.5 11.1 %copy-start.1 = (f32[32,256]{1,0:T(8,128)S(1)}, f32[32,256]{1,0:T(8,128)}, u32[]{:S(2)}) copy-start(f32[32,256]{1,0:T(8,128)} %param.15) | copy-start | bytes 98308
